TPU v7x, 512 devices: a whole 4x4x16 slice. The times are simulated.
512 devices in a mesh: ctx: 64 (over z, x), head: 8 (over y, core).
Axes of the slice: x: 4, y: 4, z: 16, core: 2. Of those that a mesh axis runs over, the one named last changes fastest.
Arguments:
- q_ret: bfloat16 [8192, 4096], P('ctx', 'head'), may hold values from -6 to 6
- k_ret: bfloat16 [8192, 4096], P('ctx', 'head'), may hold values from -6 to 6
- v_ret: bfloat16 [8192, 4096], P('ctx', 'head'), may hold values from -6 to 6
- gate_ret: bfloat16 [8192, 4096], P('ctx', 'head'), may hold values from -6 to 6
- log_decay: float32 [8192, 16], P('ctx', 'head'), may hold values from -2 to 0
- q_cross: bfloat16 [8192, 4096], P('ctx', 'head'), may hold values from -32 to 32
- cache_k: bfloat16 [8192, 2048], P(('ctx', 'head')), may hold values from -16 to 16
- cache_v: bfloat16 [8192, 2048], P(('ctx', 'head')), may hold values from -6 to 6
Outputs:
- o_ret: bfloat16 [8192, 4096], P('ctx', 'head')
- o_cross: bfloat16 [8192, 4096], P('ctx', 'head')
All inputs are finite; a program needn't handle non-finite values.
Results may differ from a plain program's by a relative error of at most 0.0039.
Values may be sent and summed in bfloat16 or wider, within the bound.
A program may use at most 128 MiB of HBM per device.

v0:
```python
import math

import jax
import jax.numpy as jnp
from jax import lax
from jax.sharding import PartitionSpec as P

HD = 256


neg_large = -1e30
norm_eps = 1e-06
highest = lax.Precision.HIGHEST


def entering(value, axis, join, neutral):
    count, mine = (lax.axis_size(axis), lax.axis_index(axis))
    pieces = jax.tree.map(lambda part: lax.all_gather(part, axis), value)
    running = jax.tree.map(
        lambda part, zero: jnp.full_like(part, 0) + jnp.asarray(zero, part.dtype), value, neutral
    )

    def lap(position, running):
        longer = join(running, jax.tree.map(lambda part: part[position], pieces))
        return jax.tree.map(lambda new, old: jnp.where(position < mine, new, old), longer, running)

    return lax.fori_loop(0, count - 1, lap, running)


def split_heads(matrix_in):
    return matrix_in.reshape(matrix_in.shape[0], matrix_in.shape[1] // HD, HD).transpose(1, 0, 2)


def join_heads(stacked):
    return stacked.transpose(1, 0, 2).reshape(stacked.shape[1], stacked.shape[0] * stacked.shape[2])


def chain_combine(earlier_part, later_part):
    return (
        earlier_part[0] * later_part[0],
        later_part[0][:, None, None] * earlier_part[1] + later_part[1],
    )


def retention_block(q_ret, k_ret, v_ret, gate_ret, log_decay):
    row_count = q_ret.shape[0]
    queries = split_heads(q_ret)
    key_heads = split_heads(k_ret)
    value_heads = split_heads(v_ret)
    decay_sum = jnp.cumsum(log_decay, axis=0).T
    scores = jnp.einsum("hrd,hsd->hrs", queries, key_heads, preferred_element_type=jnp.float32)
    position = lax.iota(jnp.int32, row_count)
    causal = position[:, None] >= position[None, :]
    spread = jnp.minimum(decay_sum[:, :, None] - decay_sum[:, None, :], 0.0)
    weight_matrix = jnp.where(causal[None], jnp.exp(spread) * scores, 0.0).astype(jnp.bfloat16)
    within_block = jnp.einsum(
        "hrs,hsd->hrd", weight_matrix, value_heads, preferred_element_type=jnp.float32
    )
    final_sum = decay_sum[:, -1]
    carried = (
        key_heads.astype(jnp.float32) * jnp.exp(final_sum[:, None] - decay_sum)[:, :, None]
    ).astype(jnp.bfloat16)
    summary = jnp.einsum("hsd,hse->hde", carried, value_heads, preferred_element_type=jnp.float32)
    total_decay = jnp.exp(final_sum)
    identity = (jnp.ones_like(total_decay), jnp.zeros_like(summary))
    prior_decay, prior_state = entering((total_decay, summary), "ctx", chain_combine, identity)
    from_before = jnp.einsum(
        "hrd,hde->hre", queries.astype(jnp.float32), prior_state, precision=highest
    )
    retained = within_block + jnp.exp(decay_sum)[:, :, None] * from_before
    normed = retained * lax.rsqrt(jnp.mean(retained * retained, axis=2, keepdims=True) + norm_eps)
    gated_out = normed * jax.nn.silu(split_heads(gate_ret).astype(jnp.float32))
    return join_heads(gated_out).astype(jnp.bfloat16)


def pick_block(length):
    size_now = min(length, 1024)
    while length % size_now != 0:
        size_now = size_now - 1
    return size_now


def attend_keys(state_now, key_block, value_block, offset, flat_queries, row_position, score_scale):
    top_score, run_total, running_sum = state_now
    scores = (
        jnp.einsum("rd,kd->rk", flat_queries, key_block, preferred_element_type=jnp.float32)
        * score_scale
    )
    key_position = offset + lax.iota(jnp.int32, key_block.shape[0])
    allowed = row_position[:, None] >= key_position[None, :]
    masked = jnp.where(allowed, scores, neg_large)
    new_top = jnp.maximum(top_score, jnp.max(masked, axis=1))
    weight_matrix = jnp.where(allowed, jnp.exp(masked - new_top[:, None]), 0.0)
    rescale = jnp.exp(top_score - new_top)
    run_total = run_total * rescale + jnp.sum(weight_matrix, axis=1)
    running_sum = running_sum * rescale[:, None] + jnp.dot(
        weight_matrix.astype(jnp.bfloat16), value_block, preferred_element_type=jnp.float32
    )
    return (new_top, run_total, running_sum)


def fold_piece(carries, cache_piece, query_sets, score_scale):
    key_piece, value_piece = cache_piece
    length = key_piece.shape[0]
    size_now = pick_block(length)
    blocks = length // size_now
    key_blocks = key_piece.reshape(blocks, size_now, key_piece.shape[1])
    value_blocks = value_piece.reshape(blocks, size_now, value_piece.shape[1])
    offsets = size_now * lax.iota(jnp.int32, blocks)
    results = []
    for carry_one, query_set in zip(carries, query_sets):
        flat_queries, row_position = query_set
        last_query = jnp.max(row_position)

        def one_block(state_now, inputs):
            key_block, value_block, offset = inputs

            def active(current):
                return attend_keys(
                    current, key_block, value_block, offset, flat_queries, row_position, score_scale
                )

            def passive(current):
                return current

            return (lax.cond(offset <= last_query, active, passive, state_now), None)

        carry_one, unused = lax.scan(one_block, carry_one, (key_blocks, value_blocks, offsets))
        results.append(carry_one)
    return tuple(results)


def make_queries(q_block, first_position):
    head_count = q_block.shape[1] // HD
    flat_queries = split_heads(q_block).reshape(head_count * q_block.shape[0], HD)
    position = first_position + lax.iota(jnp.int32, q_block.shape[0])
    return (flat_queries, jnp.tile(position, head_count))


def start_state(row_total):
    return (
        jnp.full((row_total,), neg_large, jnp.float32),
        jnp.zeros((row_total,), jnp.float32),
        jnp.zeros((row_total, HD), jnp.float32),
    )


def finish(state_now, head_count):
    top_score, run_total, running_sum = state_now
    mixed_out = running_sum / run_total[:, None]
    row_count = mixed_out.shape[0] // head_count
    return join_heads(mixed_out.reshape(head_count, row_count, HD)).astype(jnp.bfloat16)


def per_device(q_ret, k_ret, v_ret, gate_ret, log_decay, q_cross, cache_k, cache_v):
    o_ret = retention_block(q_ret, k_ret, v_ret, gate_ret, log_decay)
    key_rows, value_rows = (
        lax.all_to_all(cache_k, "head", split_axis=1, concat_axis=0, tiled=True),
        lax.all_to_all(cache_v, "head", split_axis=1, concat_axis=0, tiled=True),
    )
    row_count = q_cross.shape[0]
    head_count = q_cross.shape[1] // HD
    score_scale = 1.0 / math.sqrt(HD)
    index_ctx = lax.axis_index("ctx")
    first_row = index_ctx * row_count
    query_sets = (make_queries(q_cross, first_row),)
    initial = tuple(
        (start_state(flat_queries.shape[0]) for flat_queries, row_position in query_sets)
    )
    states = fold_piece(
        initial,
        (
            lax.all_gather(key_rows, "ctx", axis=0, tiled=True),
            lax.all_gather(value_rows, "ctx", axis=0, tiled=True),
        ),
        query_sets,
        score_scale,
    )
    o_cross = finish(states[0], head_count)
    return (o_ret, o_cross)


def solution(mesh):
    placed = (
        P("ctx", "head"),
        P("ctx", "head"),
        P("ctx", "head"),
        P("ctx", "head"),
        P("ctx", "head"),
        P("ctx", "head"),
        P(("ctx", "head"), None),
        P(("ctx", "head"), None),
    )
    return jax.shard_map(
        per_device,
        mesh=mesh,
        in_specs=placed,
        out_specs=(P("ctx", "head"), P("ctx", "head")),
        check_vma=False,
    )
```

profile of v0, /device:TPU:1, one launch (start us, length us, event | category | flops | bytes accessed | tf_op | source)
XLA Modules:
  0.0 686.4 jit_solution(15930455387534163485)
XLA Ops:
  8.1 14.7 %all_to_all.38 = bf16[16,8,256]{2,0,1:T(8,128)(2,1)} all-to-all(bf16[16,8,256]{2,0,1:T(8,128)(2,1)S(1)} %bitcast.128), channel_id=1, replica_groups=mesh['ctx'=64,'head'=8] {'head'}, dimensions={1} | all-to-all | bytes 131072 | tf_op jit(solution)/shard_map/all_to_all | solution.py:158
  23.7 8.7 %all_to_all.39 = bf16[16,8,256]{2,0,1:T(8,128)(2,1)} all-to-all(bf16[16,8,256]{2,0,1:T(8,128)(2,1)S(1)} %bitcast.129), channel_id=1, replica_groups=mesh['ctx'=64,'head'=8] {'head'}, dimensions={1} | all-to-all | bytes 131072 | tf_op jit(solution)/shard_map/all_to_all | solution.py:159
  34.8 1.9 fusion.28
  36.8 1.3 dynamic-slice
  39.0 118.2 %all-reduce = f32[128]{0:T(128)S(1)} all-reduce(f32[128]{0:T(128)S(1)} %dynamic-update-slice), channel_id=2, replica_groups=mesh['ctx'=64,'head'=8] {'ctx'}, use_global_device_ids=true, to_apply=%add | all-reduce | flops 128 | bytes 1024
  160.2 142.3 %all-gather.8.cloned.1.call-done = bf16[8192,256]{1,0:T(8,128)(2,1)} async-done(((bf16[128,256]{1,0:T(8,128)(2,1)}), bf16[8192,256]{1,0:T(8,128)(2,1)}) %all-gather.8.cloned.1.call-update) | async-done | bytes 4194320 | tf_op jit(solution)/shard_map/all_gather | solution.py:174
  302.5 19.5 %while.29 = (s32[]{:T(128)}, f32[256]{0:T(256)S(1)}, f32[256]{0:T(256)S(1)}, f32[256,256]{1,0:T(8,128)S(1)}, s32[8]{0:T(128)S(1)}, /*index=5*/s32[]{:T(128)}, bf...) while((s32[]{:T(128)}, f32[256]{0:T(256)S(1)}, ...), condition=%wide.region_10.11_spmd.clone, body=%wide.region_5.10_spmd.clone.sunk | while | flops 271713792 | bytes 4888331 | solution.py:128
  304.4 4.1 conditional.3
  305.1 1.4 fusion.44
  306.8 1.7 convolution_add_fusion
  323.0 278.7 %all-gather.10.cloned.1.call-done = f32[128,256,256]{2,1,0:T(8,128)} async-done(((f32[2,256,256]{2,1,0:T(8,128)}), f32[128,256,256]{2,1,0:T(8,128)}) %all-gather.10.cloned.1.call-update) | async-done | bytes 33554448 | tf_op jit(solution)/shard_map/all_gather | solution.py:18
  601.7 76.3 %while.30 = (s32[]{:T(128)}, f32[2,256,256]{2,1,0:T(8,128)S(1)}, s32[]{:T(128)}, f32[64,2]{1,0:T(8,128)S(1)}, f32[64,2,256,256]{3,2,1,0:T(8,128)}, /*index=5*/s32[]{:T(128)}, s32[]{:T(128)}) while((s32[]{:T(128)}, f32[2,256,256]{2,1,0:T(8,128)S(1)}, s32[]{:T(128)}, f32[64,2]{1,0:T(8,128)S(1)}, f32[64,2,256,256]{3,2,1,0:T(8,128)}, ...), condition=%wide.region_2.3_spmd.clone, body=%wide.region_1.2_spmd.clone.sunk | while | flops 524292 | bytes 1572993 | solution.py:27
  601.7 1.2 fusion.49
  602.9 1.2 fusion.49
  612.6 1.2 fusion.49
  613.9 1.2 fusion.49
  615.1 1.2 fusion.49
  616.3 1.2 fusion.49
  617.5 1.2 fusion.49
  618.7 1.2 fusion.49
  635.7 1.2 fusion.49
  636.9 1.2 fusion.49
  638.1 1.2 fusion.49
  639.3 1.2 fusion.49
  640.5 1.2 fusion.49
  641.7 1.2 fusion.49
  658.7 1.2 fusion.49
  659.9 1.2 fusion.49
  661.1 1.2 fusion.49
  662.3 1.2 fusion.49
  663.5 1.2 fusion.49
  664.7 1.2 fusion.49
  (171 shorter events, 66.9 us)
Async XLA Ops:
  7.2 153.0 %all-gather.6.cloned.1.call-start = ((), (), s32[]{:S(2)}) async-start(), calls=%async_computation.2 | async-start | bytes 4259840 | tf_op jit(solution)/shard_map/all_gather | solution.py:173
  22.8 279.7 %all-gather.8.cloned.1.call-start = ((), (), s32[]{:S(2)}) async-start(), calls=%async_computation.3 | async-start | bytes 4259840 | tf_op jit(solution)/shard_map/all_gather | solution.py:174
  32.4 569.3 %all-gather.10.cloned.1.call-start = ((), (), s32[]{:S(2)}) async-start(), calls=%async_computation.4 | async-start | bytes 34078720 | tf_op jit(solution)/shard_map/all_gather | solution.py:18
  322.3 355.8 %copy-start = (bf16[128,512]{1,0:T(8,128)(2,1)S(1)}, bf16[128,512]{1,0:T(8,128)(2,1)}, u32[]{:S(2)}) copy-start(bf16[128,512]{1,0:T(8,128)(2,1)} %param.14) | copy-start | bytes 393220
  601.7 76.7 %copy-start.1 = (bf16[128,512]{1,0:T(8,128)(2,1)S(1)}, bf16[128,512]{1,0:T(8,128)(2,1)}, u32[]{:S(2)}) copy-start(bf16[128,512]{1,0:T(8,128)(2,1)} %param.16) | copy-start | bytes 393220
Sparse Core Ops, SparseCore 0:
  22.9 135.4 all-gather.5
  161.4 141.0 all-gather.7
  305.4 296.2 all-gather.9
where the time goes:
time: 691 us; the launch traced here: 686 us
  waiting for transfers between devices  421 us (61%)
  blocking collectives  142 us (21%)
  other arithmetic  75.8 us (11%)
  local copies, waits for them, and re-layouts  14.8 us (2%)
  between operations  14.6 us (2%)
  loops' own time  12.6 us (2%)
    all_gather x1, waiting for transfers between devices, entering(): pieces = jax.tree.map(lambda part: lax.all_gather(part, axis), value)  279 us
    all_gather x1, waiting for transfers between devices, per_device(): lax.all_gather(value_rows, 'ctx', axis=0, tiled=True)  142 us
    unnamed x1, blocking collectives  118 us
    select_n x63, other arithmetic, lap(): jnp.where(position < mine, new, old)  73.8 us
    all_to_all x1, blocking collectives, per_device(): lax.all_to_all(cache_k, 'head', split_axis=1, concat_axis=0, tiled=True)  14.7 us
  transfers between devices with their start and end apart: 3, of which 2 were waited for; matrix products, arithmetic and copies ran while one was open for 3% of the time, Pallas kernels for 0%

commit v1 on v0

v1 whole, which is shorter than its diff:
```python
import functools
import math

import jax
import jax.numpy as jnp
from jax import lax
from jax.experimental import pallas as pl
from jax.experimental.pallas import tpu as pltpu
from jax.sharding import PartitionSpec as P

HD = 256
X = 4
NEG = -1e30
EPS = 1e-06
MESH = pl.DeviceIdType.MESH
bf16, f32 = jnp.bfloat16, jnp.float32
SCALE2 = math.log2(math.e) / math.sqrt(HD)
NT = (((1,), (1,)), ((), ()))
TN = (((0,), (0,)), ((), ()))


def mm(a, b, dims=(((1,), (0,)), ((), ()))):
    return lax.dot_general(a, b, dims, preferred_element_type=f32)


def wide(a):
    return jnp.concatenate([a, a], axis=1)


def kernel(
    Z, NH, T,
    q_ret, k_ret, v_ret, gate, ld, q_x, cache_k, cache_v,
    o_ret, o_x,
    qbuf, own, kv, gown, gbuf, m_s, l_s, acc, o_send, o_recv, st_send, st_recv,
    d_s, within, silu, sum_send, sum_recv, t_send, t_recv, qr, s_f, s_b, e_f,
    fb_send, fb_recv,
    loc_sem, c_send, c_recv, x_send, x_recv, z_send, z_recv,
):
    F = Z // 2
    B = F - 1
    RP = T // NH
    c = lax.axis_index("ctx")
    h = lax.axis_index("head")
    z = lax.div(c, X)
    x = lax.rem(c, X)
    plane = z * X

    def xdev(r):
        xp = lax.rem(x + r, X)
        return xp, (plane + xp, h)

    def hdev(r):
        hp = lax.rem(h + r, NH)
        return hp, (c, hp)

    up = (lax.rem(c + X, Z * X), h)
    down = (lax.rem(c + (Z - 1) * X, Z * X), h)

    def remote(src, dst, ss, rs, dev):
        return pltpu.make_async_remote_copy(
            src_ref=src, dst_ref=dst, send_sem=ss, recv_sem=rs,
            device_id=dev, device_id_type=MESH,
        )

    barrier = pltpu.get_barrier_semaphore()
    for r in range(1, NH):
        pl.semaphore_signal(barrier, inc=1, device_id=hdev(r)[1], device_id_type=MESH)
    for r in range(1, X):
        pl.semaphore_signal(barrier, inc=1, device_id=xdev(r)[1], device_id_type=MESH)
    pl.semaphore_signal(barrier, inc=1, device_id=up, device_id_type=MESH)
    pl.semaphore_signal(barrier, inc=1, device_id=down, device_id_type=MESH)

    def head_cols(i):
        return pl.ds(pl.multiple_of(i * HD, HD), HD)

    locals_ = [
        pltpu.make_async_copy(cache_k.at[:, head_cols(h)], own.at[0, pl.ds(pl.multiple_of(h * RP, RP), RP)], loc_sem.at[0]),
        pltpu.make_async_copy(cache_v.at[:, head_cols(h)], own.at[1, pl.ds(pl.multiple_of(h * RP, RP), RP)], loc_sem.at[1]),
        pltpu.make_async_copy(q_x.at[:, 0:HD], qbuf.at[x, 0], loc_sem.at[2]),
        pltpu.make_async_copy(q_x.at[:, HD:2 * HD], qbuf.at[x, 1], loc_sem.at[3]),
        pltpu.make_async_copy(q_ret.at[:, head_cols(lax.div(x, 2))], qr.at[x], loc_sem.at[4]),
    ]
    for cp in locals_:
        cp.start()

    rows = lax.broadcasted_iota(jnp.int32, (T, T), 0)
    cols = lax.broadcasted_iota(jnp.int32, (T, T), 1)
    for hh in range(2):
        d = jnp.broadcast_to(ld[:, hh:hh + 1], (T, T))
        step = 1
        while step < T:
            d = d + jnp.where(rows >= step, pltpu.roll(d, step, 0), 0.0)
            step *= 2
        d_s[hh] = d
        last = d[T - 1:T, :]
        fade = jnp.exp(last - d)
        kh = k_ret[:, hh * HD:(hh + 1) * HD]
        vh = v_ret[:, hh * HD:(hh + 1) * HD]
        carried = (kh.astype(f32) * wide(fade)).astype(bf16)
        summ = mm(carried, vh, TN)
        sum_send[2 * hh] = summ[:, :HD // 2]
        sum_send[2 * hh + 1] = summ[:, HD // 2:]
        t_send[4 * hh:4 * hh + 4, :] = jnp.broadcast_to(last, (4, T))

    pl.semaphore_wait(barrier, (NH - 1) + (X - 1) + 2)

    def cache_copy(r, t):
        src = cache_k if t == 0 else cache_v
        hp, dev = hdev(r)
        return remote(
            src.at[:, head_cols(hp)], own.at[t, pl.ds(pl.multiple_of(h * RP, RP), RP)],
            c_send.at[t, r], c_recv.at[t, r], dev,
        )

    for r in range(1, NH):
        for t in range(2):
            cache_copy(r, t).start()

    def x_copy(kind, r):
        xp, dev = xdev(r)
        if kind == 0:
            src, dst = sum_send.at[xp], sum_recv.at[x]
        elif kind == 1:
            src, dst = t_send, t_recv.at[x]
        elif kind == 2 or kind == 3:
            src, dst = q_x.at[:, (kind - 2) * HD:(kind - 1) * HD], qbuf.at[x, kind - 2]
        elif kind == 4:
            src, dst = q_ret.at[:, head_cols(lax.div(xp, 2))], qr.at[x]
        elif kind == 5:
            src, dst = o_send.at[xp], o_recv.at[x]
        elif kind == 6:
            src, dst = st_send.at[xp], st_recv.at[x]
        else:
            src, dst = fb_send.at[xp], fb_recv.at[x]
        return remote(src, dst, x_send.at[kind, r], x_recv.at[kind, r], dev)

    order = (2, 1, 3)
    for kind in (1, 0, 2, 3, 4):
        for r in order:
            x_copy(kind, r).start()

    sum_recv[x] = sum_send[x]
    t_recv[x] = t_send[...]
    for hh in range(2):
        d = d_s[hh]
        qh = q_ret[:, hh * HD:(hh + 1) * HD]
        kh = k_ret[:, hh * HD:(hh + 1) * HD]
        vh = v_ret[:, hh * HD:(hh + 1) * HD]
        spread = jnp.minimum(d - d.T, 0.0)
        w = jnp.where(rows >= cols, jnp.exp(spread) * mm(qh, kh, NT), 0.0).astype(bf16)
        within[hh] = mm(w, vh)
        g = gate[:, hh * HD:(hh + 1) * HD].astype(f32)
        silu[hh] = g / (1.0 + jnp.exp(-g))

    def slot(t, way, i):
        return gbuf.at[way, i] if t == 2 else kv.at[t, way, i]

    def mine(t):
        return gown if t == 2 else own.at[t]

    def send_own(t, way):
        return remote(mine(t), slot(t, way, 0), z_send.at[t, way, 0], z_recv.at[t, way, 0], up if way == 0 else down)

    back_shift = jnp.where(z < F, 1, 0)

    def pass_on(t, way, i):
        to = i + 1 if way == 0 else i + back_shift
        return remote(slot(t, way, i), slot(t, way, to), z_send.at[t, way, i + 1], z_recv.at[t, way, to], up if way == 0 else down)

    own_up = z < Z - 1
    own_down = z < B
    got_up = jnp.minimum(z, F)
    got_down = jnp.where(z < F, jnp.maximum(B - 1 - z, 0), z - F)
    use_down = jnp.where(z < F, 0, z - F)
    pass_up = jnp.where(z < Z - 1, jnp.minimum(z, F - 1), 0)
    pass_down = jnp.where(z < F, got_down, jnp.maximum(z - F - 1, 0))

    def start_own(t):
        @pl.when(own_up)
        def _():
            send_own(t, 0).start()

        @pl.when(own_down)
        def _():
            send_own(t, 1).start()

    locals_[0].wait()
    locals_[1].wait()
    for t in range(2):
        for r in range(1, NH):
            cache_copy(r, t).wait_recv()
        start_own(t)

    for kind in (1, 0):
        for r in order:
            x_copy(kind, (X - r) % X).wait_recv()

    second = lax.div(x, 2) == 1

    def total(i):
        tr = t_recv[i]
        return jnp.where(second, tr[4:5, :], tr[0:1, :])

    g = sum_recv[0]
    plane_sum = total(0)
    for i in range(1, X):
        g = g * jnp.exp(total(i)) + sum_recv[i]
        plane_sum = plane_sum + total(i)
    gown[0:HD, :] = g.astype(bf16)
    hi = plane_sum.astype(bf16)
    rest = plane_sum - hi.astype(f32)
    mid = rest.astype(bf16)
    low = (rest - mid.astype(f32)).astype(bf16)
    tail_rows = lax.broadcasted_iota(jnp.int32, (16, HD // 2), 0)
    gown[HD:HD + 16, :] = jnp.where(
        tail_rows == 0, hi.astype(f32), jnp.where(tail_rows == 1, mid.astype(f32), jnp.where(tail_rows == 2, low.astype(f32), 0.0))
    ).astype(bf16)
    start_own(2)

    for kind in (2, 3):
        locals_[kind].wait()
        for r in order:
            x_copy(kind, r).wait_recv()

    def attend(kb, vb, first):
        k = kb[...]
        v = vb[...]
        for i in range(X):
            q = qbuf[i].reshape(2 * T, HD)
            at = pl.ds(i * 2 * T, 2 * T)
            s = mm(q, k, NT)
            if first:
                t_pos = lax.rem(lax.broadcasted_iota(jnp.int32, (2 * T, T), 0), T)
                ok = t_pos + (i - x) * T >= lax.broadcasted_iota(jnp.int32, (2 * T, T), 1)
                s = jnp.where(ok, s, NEG)
                m_new = jnp.broadcast_to(jnp.max(s, axis=1, keepdims=True), (2 * T, T))
                p = jnp.where(ok, jnp.exp2((s - m_new) * SCALE2), 0.0)
                l_s[at, :] = p
                acc[at, :] = mm(p.astype(bf16), v)
            else:
                m_old = m_s[at, :]
                m_new = jnp.maximum(m_old, jnp.max(s, axis=1, keepdims=True))
                p = jnp.exp2((s - m_new) * SCALE2)
                alpha = jnp.exp2((m_old - m_new) * SCALE2)
                l_s[at, :] = l_s[at, :] * alpha + p
                acc[at, :] = acc[at, :] * wide(alpha) + mm(p.astype(bf16), v)
            m_s[at, :] = m_new

    attend(own.at[0], own.at[1], True)
    s_f[...] = jnp.zeros_like(s_f)
    s_b[...] = jnp.zeros_like(s_b)
    e_f[...] = jnp.zeros_like(e_f)

    def plane_decay(way, i):
        tail = gbuf[way, i, HD:HD + 16, :].astype(f32)
        return tail[0:1, :] + tail[1:2, :] + tail[2:3, :]

    def receive(way, i, got, passed):
        for t in range(3):
            @pl.when(i < got)
            def _():
                remote(mine(t), slot(t, way, i), z_send.at[t, way, 0], z_recv.at[t, way, i], up if way == 0 else down).wait_recv()

            @pl.when(i < passed)
            def _():
                pass_on(t, way, i).start()

    def step(i, carry):
        receive(0, i, got_up, pass_up)
        receive(1, i, got_down, pass_down)

        @pl.when(i < got_up)
        def _():
            attend(kv.at[0, 0, i], kv.at[1, 0, i], False)
            s_f[...] = s_f[...] + jnp.exp(e_f[0:1, :]) * gbuf[0, i, 0:HD, :].astype(f32)
            e_f[...] = e_f[...] + plane_decay(0, i)

        @pl.when(i < use_down)
        def _():
            attend(kv.at[0, 1, i], kv.at[1, 1, i], False)
            s_b[...] = s_b[...] * jnp.exp(plane_decay(1, i)) + gbuf[1, i, 0:HD, :].astype(f32)

        return carry

    lax.fori_loop(0, F, step, 0)

    locals_[4].wait()
    for r in order:
        x_copy(4, r).wait_recv()
    state = s_f[...] + jnp.exp(e_f[0:1, :]) * s_b[...]
    for i in range(X):
        top = state.astype(bf16)
        low_part = (state - top.astype(f32)).astype(bf16)
        fb_send[i] = mm(qr[i], top) + mm(qr[i], low_part)
        if i < X - 1:
            state = state * jnp.exp(total(i)) + sum_recv[i]
    for r in order:
        x_copy(7, r).start()

    lane = lax.broadcasted_iota(jnp.int32, (T, T), 1)
    for r in order:
        xp, _ = xdev(r)
        stat = jnp.zeros((T, T), f32)
        for hh in range(2):
            at = pl.ds(pl.multiple_of((xp * 2 + hh) * T, T), T)
            l = jnp.sum(l_s[at, :], axis=1, keepdims=True)
            o_send[xp, hh] = (acc[at, :] / jnp.where(l > 0.0, l, 1.0)).astype(bf16)
            stat = jnp.where(lane == 2 * hh, m_s[at, :], stat)
            stat = jnp.where(lane == 2 * hh + 1, l, stat)
        st_send[xp] = stat.T[0:8, :]
        x_copy(6, r).start()
        x_copy(5, r).start()

    for r in order:
        x_copy(7, r).wait_recv()
    fb_recv[x] = fb_send[x]
    for hh in range(2):
        d = jnp.exp(d_s[hh])
        before = jnp.concatenate([fb_recv[2 * hh], fb_recv[2 * hh + 1]], axis=1)
        kept = within[hh] + wide(d) * before
        normed = kept * lax.rsqrt(jnp.mean(kept * kept, axis=1, keepdims=True) + EPS)
        o_ret[:, hh * HD:(hh + 1) * HD] = (normed * silu[hh]).astype(bf16)

    for kind in (6, 5):
        for r in order:
            x_copy(kind, r).wait_recv()
    stats = {}
    for r in order:
        xp, _ = xdev(r)
        stats[r] = (xp, jnp.concatenate([st_recv[xp]] * (T // 8), axis=0).T)
    for hh in range(2):
        at = pl.ds(pl.multiple_of((x * 2 + hh) * T, T), T)
        m_own = m_s[at, :][:, 0:1]
        l_own = jnp.sum(l_s[at, :], axis=1, keepdims=True)
        top = m_own
        for r in order:
            top = jnp.maximum(top, stats[r][1][:, 2 * hh:2 * hh + 1])
        w_own = jnp.exp2((m_own - top) * SCALE2)
        out = acc[at, :] * w_own
        weight = l_own * w_own
        for r in order:
            xp, st = stats[r]
            w = jnp.exp2((st[:, 2 * hh:2 * hh + 1] - top) * SCALE2) * st[:, 2 * hh + 1:2 * hh + 2]
            out = out + o_recv[xp, hh].astype(f32) * w
            weight = weight + w
        o_x[:, hh * HD:(hh + 1) * HD] = (out / weight).astype(bf16)

    for r in range(1, NH):
        for t in range(2):
            cache_copy(r, t).wait_send()
    for kind in range(8):
        for r in order:
            x_copy(kind, r).wait_send()
    for t in range(3):
        @pl.when(own_up)
        def _():
            send_own(t, 0).wait_send()

        @pl.when(own_down)
        def _():
            send_own(t, 1).wait_send()

    def drain(i, carry):
        for t in range(3):
            @pl.when(i < pass_up)
            def _():
                pass_on(t, 0, i).wait_send()

            @pl.when(i < pass_down)
            def _():
                pass_on(t, 1, i).wait_send()
        return carry

    lax.fori_loop(0, F, drain, 0)


def per_device(Z, NH, *args):
    T = args[0].shape[0]
    F = Z // 2
    W = HD // 2
    vm = pltpu.VMEM
    dma = pltpu.SemaphoreType.DMA
    out = jax.ShapeDtypeStruct((T, 2 * HD), bf16)
    return pl.pallas_call(
        functools.partial(kernel, Z, NH, T),
        out_shape=(out, out),
        in_specs=[pl.BlockSpec(memory_space=pltpu.VMEM)] * 8,
        out_specs=(pl.BlockSpec(memory_space=pltpu.VMEM),) * 2,
        scratch_shapes=[
            vm((X, 2, T, HD), bf16), vm((2, T, HD), bf16), vm((2, 2, F, T, HD), bf16),
            vm((HD + 16, W), bf16), vm((2, F, HD + 16, W), bf16),
            vm((X * 2 * T, T), f32), vm((X * 2 * T, T), f32), vm((X * 2 * T, HD), f32),
            vm((X, 2, T, HD), bf16), vm((X, 2, T, HD), bf16), vm((X, 8, T), f32), vm((X, 8, T), f32),
            vm((2, T, T), f32), vm((2, T, HD), f32), vm((2, T, HD), f32),
            vm((4, HD, W), f32), vm((X, HD, W), f32), vm((8, T), f32), vm((X, 8, T), f32),
            vm((X, T, HD), bf16), vm((HD, W), f32), vm((HD, W), f32), vm((8, T), f32),
            vm((X, T, W), f32), vm((X, T, W), f32),
            dma((5,)), dma((2, NH)), dma((2, NH)), dma((8, X)), dma((8, X)),
            dma((3, 2, F + 1)), dma((3, 2, F + 1)),
        ],
        compiler_params=pltpu.CompilerParams(collective_id=0, has_side_effects=True),
        name="block",
    )(*args)


def solution(mesh):
    Z, NH = mesh.shape["ctx"] // X, mesh.shape["head"]
    split = P("ctx", "head")
    rows = P(("ctx", "head"), None)
    return jax.shard_map(
        functools.partial(per_device, Z, NH),
        mesh=mesh,
        in_specs=(split,) * 6 + (rows,) * 2,
        out_specs=(split, split),
        check_vma=False,
    )
```

time: 691 us -> 89.2 us (0.13)
  the two profiles are of different devices: /device:TPU:1 before, /device:TPU:448 now
where the time goes in v1:
time: 89.2 us; the launch traced here: 89 us
  Pallas kernels  84.7 us (95%)
  local copies, waits for them, and re-layouts  3.68 us (4%)
    pallas_call x1, Pallas kernels, per_device(): pl.pallas_call(functools.partial(kernel, Z, NH, T), out_shape=(out, out),...  84.7 us
    unnamed x5, local copies, waits for them, and re-layouts  3.68 us

profile of v1, /device:TPU:448, one launch (start us, length us, event | category | flops | bytes accessed | tf_op | source)
XLA Modules:
  0.0 89.0 jit_solution(9107919624035121387)
XLA Ops:
  0.6 1.4 %copy.10.ld = f32[128,2]{1,0:T(8,128)} copy(f32[128,2]{0,1:T(2,128)} %param.12) | data formatting | bytes 2048 | tf_op args[4]
  2.0 84.7 %block.1 = (bf16[128,512]{1,0:T(8,128)(2,1)}, bf16[128,512]{1,0:T(8,128)(2,1)}) custom-call(bf16[128,512]{1,0:T(8,128)(2,1)} %q_ret.1, bf16[128,512]{1,0:T(8,128)(2,1)} %k_ret.1, bf16[128,512]{1,0:T(8,128)(2,1)} %v_ret.1, bf16[128,512]{1,0:T(8,128)(2,1)} %gate.1, f32[128,2]{1,0:T(8,128)} %copy.10.ld, bf16[128,512]{1,0:T(8,128)(2,1)} %q_x.1, ...), custom_call_target="tpu_custom_call" | custom-call | tf_op jit(solution)/shard_map/block/pallas_call | solution.py:384
  86.8 0.0 copy-start
  86.8 1.6 %copy.13 = bf16[128,512]{1,0:T(8,128)(2,1)} copy(bf16[128,512]{1,0:T(8,128)(2,1)} %get-tuple-element.4) | data formatting | bytes 262144
  88.4 0.0 copy-done
  88.4 0.7 copy.14
Async XLA Ops:
  86.8 1.6 %copy-start = (bf16[128,512]{1,0:T(8,128)(2,1)S(1)}, bf16[128,512]{1,0:T(8,128)(2,1)}, u32[]{:S(2)}) copy-start(bf16[128,512]{1,0:T(8,128)(2,1)} %get-tuple-element.5) | copy-start | bytes 393220

commit v2 on v1

v2 whole, which is shorter than its diff:
```python
import functools
import math

import jax
import jax.numpy as jnp
from jax import lax
from jax.experimental import pallas as pl
from jax.experimental.pallas import tpu as pltpu
from jax.sharding import PartitionSpec as P

HD = 256
X = 4
NEG = -1e30
EPS = 1e-06
MESH = pl.DeviceIdType.MESH
bf16, f32 = jnp.bfloat16, jnp.float32
SCALE2 = math.log2(math.e) / math.sqrt(HD)
NT = (((1,), (1,)), ((), ()))
TN = (((0,), (0,)), ((), ()))


def mm(a, b, dims=(((1,), (0,)), ((), ()))):
    return lax.dot_general(a, b, dims, preferred_element_type=f32)


def wide(a):
    return jnp.concatenate([a, a], axis=1)


def kernel(
    Z, NH, T,
    q_ret, k_ret, v_ret, gate, ld, q_x, cache_k, cache_v,
    o_ret, o_x,
    qv, kvv, vv, gv, ldv,
    qbuf, own, kv, gown, gsingle, gpair, gbuf, m_s, l_s, acc, o_send, o_recv, st_send, st_recv,
    d_s, within, silu, sum_send, sum_recv, t_send, t_recv, qr, s_f, s_b, e_f,
    fb_send, fb_recv,
    loc_sem, c_send, c_recv, x_send, x_recv, z_send, z_recv, g_send, g_recv,
):
    F = Z // 2
    B = F - 1
    RP = T // NH
    HALF = HD // 2
    c = lax.axis_index("ctx")
    h = lax.axis_index("head")
    z = lax.div(c, X)
    x = lax.rem(c, X)
    odd = lax.rem(z, 2)
    plane = z * X

    def xdev(r):
        xp = lax.rem(x + r, X)
        return xp, (plane + xp, h)

    def hdev(r):
        hp = lax.rem(h + r, NH)
        return hp, (c, hp)

    up = (lax.rem(c + X, Z * X), h)
    down = (lax.rem(c + (Z - 1) * X, Z * X), h)

    def remote(src, dst, ss, rs, dev):
        return pltpu.make_async_remote_copy(
            src_ref=src, dst_ref=dst, send_sem=ss, recv_sem=rs,
            device_id=dev, device_id_type=MESH,
        )

    barrier = pltpu.get_barrier_semaphore()
    for r in range(1, NH):
        pl.semaphore_signal(barrier, inc=1, device_id=hdev(r)[1], device_id_type=MESH)
    for r in range(1, X):
        pl.semaphore_signal(barrier, inc=1, device_id=xdev(r)[1], device_id_type=MESH)
    pl.semaphore_signal(barrier, inc=1, device_id=up, device_id_type=MESH)
    pl.semaphore_signal(barrier, inc=1, device_id=down, device_id_type=MESH)

    def head_cols(i):
        return pl.ds(pl.multiple_of(i * HD, HD), HD)

    my_rows = pl.ds(pl.multiple_of(h * RP, RP), RP)
    pairs = (
        (ld, ldv), (k_ret, kvv), (v_ret, vv),
        (cache_k.at[:, head_cols(h)], own.at[0, my_rows]),
        (cache_v.at[:, head_cols(h)], own.at[1, my_rows]),
        (q_ret, qv), (gate, gv),
        (q_x.at[:, 0:HD], qbuf.at[x, 0]),
        (q_x.at[:, HD:2 * HD], qbuf.at[x, 1]),
        (q_ret.at[:, head_cols(lax.div(x, 2))], qr.at[x]),
    )
    local = [pltpu.make_async_copy(src, dst, loc_sem.at[n]) for n, (src, dst) in enumerate(pairs)]
    for cp in local:
        cp.start()

    def cache_copy(r, t):
        src = cache_k if t == 0 else cache_v
        hp, dev = hdev(r)
        return remote(src.at[:, head_cols(hp)], own.at[t, my_rows], c_send.at[t, r], c_recv.at[t, r], dev)

    def x_copy(kind, r):
        xp, dev = xdev(r)
        if kind == 0:
            src, dst = sum_send.at[xp], sum_recv.at[x]
        elif kind == 1:
            src, dst = t_send, t_recv.at[x]
        elif kind == 2 or kind == 3:
            src, dst = q_x.at[:, (kind - 2) * HD:(kind - 1) * HD], qbuf.at[x, kind - 2]
        elif kind == 4:
            src, dst = q_ret.at[:, head_cols(lax.div(xp, 2))], qr.at[x]
        elif kind == 5:
            src, dst = o_send.at[xp], o_recv.at[x]
        elif kind == 6:
            src, dst = st_send.at[xp], st_recv.at[x]
        else:
            src, dst = fb_send.at[xp], fb_recv.at[x]
        return remote(src, dst, x_send.at[kind, r], x_recv.at[kind, r], dev)

    order = (2, 1, 3)
    pl.semaphore_wait(barrier, (NH - 1) + (X - 1) + 2)
    for t in range(2):
        for r in range(1, NH):
            cache_copy(r, t).start()
    for r in (1, 3):
        x_copy(2, r).start()
        x_copy(3, r).start()

    for n in (0, 1, 2):
        local[n].wait()
    lane8 = lax.broadcasted_iota(jnp.int32, (8, T), 1)
    for hh in range(2):
        dr = jnp.broadcast_to(ldv[hh:hh + 1, :], (8, T))
        step = 1
        while step < T:
            dr = dr + jnp.where(lane8 >= step, pltpu.roll(dr, step, 1), 0.0)
            step *= 2
        d = jnp.concatenate([dr] * (T // 8), axis=0).T
        d_s[hh] = d
        last = d[T - 1:T, :]
        fade = jnp.exp(last - d)
        kh = kvv[:, hh * HD:(hh + 1) * HD]
        vh = vv[:, hh * HD:(hh + 1) * HD]
        carried = (kh.astype(f32) * wide(fade)).astype(bf16)
        summ = mm(carried, vh, TN).astype(bf16)
        sum_send[2 * hh] = summ[:, :HALF]
        sum_send[2 * hh + 1] = summ[:, HALF:]
        t_send[4 * hh:4 * hh + 4, :] = jnp.broadcast_to(last, (4, T))
    for kind in (1, 0):
        for r in order:
            x_copy(kind, r).start()
    for kind, r in ((2, 2), (3, 2), (4, 2), (4, 1), (4, 3)):
        x_copy(kind, r).start()

    def way_dev(way):
        return up if way == 0 else down

    def send_own(t, way):
        return remote(own.at[t], kv.at[t, way, 0], z_send.at[t, way, 0], z_recv.at[t, way, 0], way_dev(way))

    low = z < F
    back_shift = jnp.where(low, 1, 0)
    back_lag = jnp.where(low, 0, Z - 1 - z)

    def pass_on(t, way, i):
        to = i + 1 if way == 0 else i + back_shift
        return remote(kv.at[t, way, i], kv.at[t, way, to], z_send.at[t, way, i + 1], z_recv.at[t, way, to], way_dev(way))

    def arrival(t, way, i):
        return remote(own.at[t], kv.at[t, way, i], z_send.at[t, way, 0], z_recv.at[t, way, i], way_dev(way))

    own_up = z < Z - 1
    own_down = z < B
    got_up = jnp.minimum(z, F)
    got_down = jnp.where(low, jnp.maximum(B - 1 - z, 0), z - F)
    use_down = jnp.where(low, 0, z - F)
    pass_up = jnp.where(own_up, jnp.minimum(z, F - 1), 0)
    pass_down = jnp.where(low, got_down, jnp.maximum(z - F - 1, 0))

    def relay(t, s):
        for way in range(2):
            i = s if way == 0 else s - back_lag
            got, passed = (got_up, pass_up) if way == 0 else (got_down, pass_down)

            @pl.when(jnp.logical_and(i >= 0, i < got))
            def _():
                arrival(t, way, i).wait_recv()

            @pl.when(jnp.logical_and(i >= 0, i < passed))
            def _():
                pass_on(t, way, i).start()

    local[3].wait()
    local[4].wait()
    for t in range(2):
        for r in range(1, NH):
            cache_copy(r, t).wait_recv()

        @pl.when(own_up)
        def _():
            send_own(t, 0).start()

        @pl.when(own_down)
        def _():
            send_own(t, 1).start()

    sum_recv[x] = sum_send[x]
    t_recv[x] = t_send[...]
    s_f[...] = jnp.zeros_like(s_f)
    s_b[...] = jnp.zeros_like(s_b)
    e_f[...] = jnp.zeros_like(e_f)
    local[5].wait()
    local[6].wait()
    rows = lax.broadcasted_iota(jnp.int32, (T, T), 0)
    cols = lax.broadcasted_iota(jnp.int32, (T, T), 1)
    for hh in range(2):
        d = d_s[hh]
        qh = qv[:, hh * HD:(hh + 1) * HD]
        kh = kvv[:, hh * HD:(hh + 1) * HD]
        vh = vv[:, hh * HD:(hh + 1) * HD]
        spread = jnp.minimum(d - d.T, 0.0)
        w = jnp.where(rows >= cols, jnp.exp(spread) * mm(qh, kh, NT), 0.0).astype(bf16)
        within[hh] = mm(w, vh)
        g = gv[:, hh * HD:(hh + 1) * HD].astype(f32)
        silu[hh] = g / (1.0 + jnp.exp(-g))

    relay(0, 0)
    relay(1, 0)

    for kind in (1, 0):
        for r in order:
            x_copy(kind, r).wait_recv()

    second = lax.div(x, 2) == 1

    def total(i):
        tr = t_recv[i]
        return jnp.where(second, tr[4:5, :], tr[0:1, :])

    tail_rows = lax.broadcasted_iota(jnp.int32, (16, HALF), 0)

    def pack(ref, value, decay):
        ref[0:HD, :] = value.astype(bf16)
        hi = decay.astype(bf16).astype(f32)
        mid = (decay - hi).astype(bf16).astype(f32)
        lowest = decay - hi - mid
        rest = jnp.where(tail_rows == 0, hi, jnp.where(tail_rows == 1, mid, jnp.where(tail_rows == 2, lowest, 0.0)))
        ref[HD:HD + 16, :] = rest.astype(bf16)

    def unpack(ref):
        tail = ref[HD:HD + 16, :].astype(f32)
        return ref[0:HD, :].astype(f32), tail[0:1, :] + tail[1:2, :] + tail[2:3, :]

    g_own = sum_recv[0].astype(f32)
    g_decay = total(0)
    for i in range(1, X):
        g_own = g_own * jnp.exp(total(i)) + sum_recv[i].astype(f32)
        g_decay = g_decay + total(i)

    single = remote(gown, gsingle, g_send.at[0, F], g_recv.at[0, F], up)

    @pl.when(odd == 0)
    def _():
        pack(gown, g_own, g_decay)
        single.start()

    def pair_own(way):
        return remote(gpair, gbuf.at[way, 0], g_send.at[way, F + 1], g_recv.at[way, 0], way_dev(way))

    def pair_pass(way, k):
        to = jnp.where(low, k + odd, k) if way == 1 else k + odd
        return remote(gbuf.at[way, k], gbuf.at[way, to], g_send.at[way, k], g_recv.at[way, to], way_dev(way))

    pair_up = jnp.logical_and(odd == 1, own_up)
    pair_down = jnp.logical_and(odd == 1, own_down)
    g_up = jnp.minimum(lax.div(z, 2), jnp.where(odd == 1, F // 2, (F + 1) // 2))
    g_down = jnp.where(low, jnp.maximum(B // 2 - lax.div(z + 1, 2), 0), lax.div(jnp.maximum(z - F, 0), 2))
    g_pass_up = jnp.where(own_up, jnp.minimum(g_up, jnp.where(odd == 1, (F - 1) // 2, F // 2)), 0)
    g_pass_down = jnp.where(low, g_down, lax.div(jnp.maximum(z - 1 - F, 0), 2))

    def pair_relay(dist):
        for way in range(2):
            if way == 0:
                off = dist - 1 - odd
                got, passed = g_up, g_pass_up
            else:
                off = dist - 1 - jnp.where(low, odd, Z - z)
                got, passed = g_down, g_pass_down
            k = lax.div(jnp.maximum(off, 0), 2)
            here = jnp.logical_and(off >= 0, lax.rem(jnp.maximum(off, 0), 2) == 0)

            @pl.when(jnp.logical_and(here, k < got))
            def _():
                remote(gpair, gbuf.at[way, k], g_send.at[way, F + 1], g_recv.at[way, k], way_dev(way)).wait_recv()

            @pl.when(jnp.logical_and(here, k < passed))
            def _():
                pair_pass(way, k).start()

            if way == 0:
                @pl.when(jnp.logical_and(here, k < got))
                def _():
                    g, decay = unpack(gbuf.at[0, k])
                    s_f[...] = s_f[...] + jnp.exp(e_f[0:1, :]) * g
                    e_f[...] = e_f[...] + decay
            else:
                @pl.when(jnp.logical_and(here, jnp.logical_and(k < got, z > F)))
                def _():
                    g, decay = unpack(gbuf.at[1, k])
                    s_b[...] = s_b[...] * jnp.exp(decay) + g

    relay(0, 1)
    relay(1, 1)

    @pl.when(odd == 1)
    def _():
        remote(gown, gsingle, g_send.at[0, F], g_recv.at[0, F], up).wait_recv()
        g_before, d_before = unpack(gsingle)
        s_f[...] = g_before
        e_f[...] = e_f[...] + d_before
        pack(gpair, g_before * jnp.exp(g_decay) + g_own, d_before + g_decay)

    @pl.when(pair_up)
    def _():
        pair_own(0).start()

    @pl.when(pair_down)
    def _():
        pair_own(1).start()

    def attend(kb, vb, first):
        k = kb[...]
        v = vb[...]
        for i in range(X):
            q = qbuf[i].reshape(2 * T, HD)
            at = pl.ds(i * 2 * T, 2 * T)
            s = mm(q, k, NT)
            if first:
                t_pos = lax.rem(lax.broadcasted_iota(jnp.int32, (2 * T, T), 0), T)
                ok = t_pos + (i - x) * T >= lax.broadcasted_iota(jnp.int32, (2 * T, T), 1)
                s = jnp.where(ok, s, NEG)
                m_new = jnp.broadcast_to(jnp.max(s, axis=1, keepdims=True), (2 * T, T))
                p = jnp.where(ok, jnp.exp2((s - m_new) * SCALE2), 0.0)
                l_s[at, :] = p
                acc[at, :] = mm(p.astype(bf16), v)
            else:
                m_old = m_s[at, :]
                m_new = jnp.maximum(m_old, jnp.max(s, axis=1, keepdims=True))
                p = jnp.exp2((s - m_new) * SCALE2)
                alpha = jnp.exp2((m_old - m_new) * SCALE2)
                l_s[at, :] = l_s[at, :] * alpha + p
                acc[at, :] = acc[at, :] * wide(alpha) + mm(p.astype(bf16), v)
            m_s[at, :] = m_new

    for n in (7, 8):
        local[n].wait()
    for kind in (2, 3):
        for r in order:
            x_copy(kind, r).wait_recv()
    attend(own.at[0], own.at[1], True)

    def attend_slots(way, lo, hi):
        def one(n, carry):
            i = n if way == 0 else n - back_lag

            @pl.when(jnp.logical_and(i >= 0, i < (got_up if way == 0 else use_down)))
            def _():
                attend(kv.at[0, way, i], kv.at[1, way, i], False)

            return carry

        lax.fori_loop(lo, hi, one, 0)

    def reach(s):
        return jnp.where(s < 2, 0, jnp.where(s == 2, 1, s))

    def step(s, carry):
        lo, hi = reach(s - 1), reach(s)
        relay(0, s)
        attend_slots(0, lo, hi)
        relay(1, s)
        attend_slots(1, lo, hi)
        pair_relay(s - 1)
        return carry

    lax.fori_loop(2, F, step, 0)

    def final(n, carry):
        for way in range(2):
            attend_slots(way, n, n + 1)
        return carry

    lax.fori_loop(reach(jnp.int32(F - 1)), F, final, 0)

    lane = lax.broadcasted_iota(jnp.int32, (T, T), 1)
    for r in order:
        xp, _ = xdev(r)
        stat = jnp.zeros((T, T), f32)
        for hh in range(2):
            at = pl.ds(pl.multiple_of((xp * 2 + hh) * T, T), T)
            l = jnp.sum(l_s[at, :], axis=1, keepdims=True)
            o_send[xp, hh] = (acc[at, :] / jnp.where(l > 0.0, l, 1.0)).astype(bf16)
            stat = jnp.where(lane == 2 * hh, m_s[at, :], stat)
            stat = jnp.where(lane == 2 * hh + 1, l, stat)
        st_send[xp] = stat.T[0:8, :]
        x_copy(6, r).start()
        x_copy(5, r).start()

    def late(dist, carry):
        pair_relay(dist)
        return carry

    lax.fori_loop(F - 1, F + 1, late, 0)

    local[9].wait()
    for r in order:
        x_copy(4, r).wait_recv()
    state = s_f[...] + jnp.exp(e_f[0:1, :]) * s_b[...]
    for i in range(X):
        top = state.astype(bf16)
        low_part = (state - top.astype(f32)).astype(bf16)
        fb_send[i] = mm(qr[i], top) + mm(qr[i], low_part)
        if i < X - 1:
            state = state * jnp.exp(total(i)) + sum_recv[i].astype(f32)
    for r in order:
        x_copy(7, r).start()

    for kind in (6, 5):
        for r in order:
            x_copy(kind, r).wait_recv()
    stats = {}
    for r in order:
        xp, _ = xdev(r)
        stats[r] = (xp, jnp.concatenate([st_recv[xp]] * (T // 8), axis=0).T)
    for hh in range(2):
        at = pl.ds(pl.multiple_of((x * 2 + hh) * T, T), T)
        m_own = m_s[at, :][:, 0:1]
        l_own = jnp.sum(l_s[at, :], axis=1, keepdims=True)
        top = m_own
        for r in order:
            top = jnp.maximum(top, stats[r][1][:, 2 * hh:2 * hh + 1])
        w_own = jnp.exp2((m_own - top) * SCALE2)
        out = acc[at, :] * w_own
        weight = l_own * w_own
        for r in order:
            xp, st = stats[r]
            w = jnp.exp2((st[:, 2 * hh:2 * hh + 1] - top) * SCALE2) * st[:, 2 * hh + 1:2 * hh + 2]
            out = out + o_recv[xp, hh].astype(f32) * w
            weight = weight + w
        o_x[:, hh * HD:(hh + 1) * HD] = (out / weight).astype(bf16)

    for r in order:
        x_copy(7, r).wait_recv()
    fb_recv[x] = fb_send[x]
    for hh in range(2):
        d = jnp.exp(d_s[hh])
        before = jnp.concatenate([fb_recv[2 * hh], fb_recv[2 * hh + 1]], axis=1)
        kept = within[hh] + wide(d) * before
        normed = kept * lax.rsqrt(jnp.mean(kept * kept, axis=1, keepdims=True) + EPS)
        o_ret[:, hh * HD:(hh + 1) * HD] = (normed * silu[hh]).astype(bf16)

    for r in range(1, NH):
        for t in range(2):
            cache_copy(r, t).wait_send()
    for kind in range(8):
        for r in order:
            x_copy(kind, r).wait_send()
    for t in range(2):
        @pl.when(own_up)
        def _():
            send_own(t, 0).wait_send()

        @pl.when(own_down)
        def _():
            send_own(t, 1).wait_send()

    @pl.when(odd == 0)
    def _():
        remote(gown, gsingle, g_send.at[0, F], g_recv.at[0, F], up).wait_send()

    @pl.when(pair_up)
    def _():
        pair_own(0).wait_send()

    @pl.when(pair_down)
    def _():
        pair_own(1).wait_send()

    def drain(i, carry):
        for way, passed, g_passed in ((0, pass_up, g_pass_up), (1, pass_down, g_pass_down)):
            for t in range(2):
                @pl.when(i < passed)
                def _():
                    pass_on(t, way, i).wait_send()

            @pl.when(i < g_passed)
            def _():
                pair_pass(way, i).wait_send()
        return carry

    lax.fori_loop(0, F, drain, 0)


def per_device(Z, NH, q_ret, k_ret, v_ret, gate, log_decay, q_x, cache_k, cache_v):
    T = q_ret.shape[0]
    F = Z // 2
    W = HD // 2
    vm = pltpu.VMEM
    dma = pltpu.SemaphoreType.DMA
    out = jax.ShapeDtypeStruct((T, 2 * HD), bf16)
    item = (HD + 16, W)
    return pl.pallas_call(
        functools.partial(kernel, Z, NH, T),
        out_shape=(out, out),
        in_specs=[pl.BlockSpec(memory_space=pl.ANY)] * 8,
        out_specs=(pl.BlockSpec(memory_space=pltpu.VMEM),) * 2,
        scratch_shapes=[
            vm((T, 2 * HD), bf16), vm((T, 2 * HD), bf16), vm((T, 2 * HD), bf16), vm((T, 2 * HD), bf16), vm((2, T), f32),
            vm((X, 2, T, HD), bf16), vm((2, T, HD), bf16), vm((2, 2, F, T, HD), bf16),
            vm(item, bf16), vm(item, bf16), vm(item, bf16), vm((2, F // 2 + 1) + item, bf16),
            vm((X * 2 * T, T), f32), vm((X * 2 * T, T), f32), vm((X * 2 * T, HD), f32),
            vm((X, 2, T, HD), bf16), vm((X, 2, T, HD), bf16), vm((X, 8, T), f32), vm((X, 8, T), f32),
            vm((2, T, T), f32), vm((2, T, HD), f32), vm((2, T, HD), f32),
            vm((4, HD, W), bf16), vm((X, HD, W), bf16), vm((8, T), f32), vm((X, 8, T), f32),
            vm((X, T, HD), bf16), vm((HD, W), f32), vm((HD, W), f32), vm((8, T), f32),
            vm((X, T, W), f32), vm((X, T, W), f32),
            dma((10,)), dma((2, NH)), dma((2, NH)), dma((8, X)), dma((8, X)),
            dma((2, 2, F + 1)), dma((2, 2, F + 1)), dma((2, F + 2)), dma((2, F + 2)),
        ],
        compiler_params=pltpu.CompilerParams(collective_id=0, has_side_effects=True),
        name="block",
    )(q_ret, k_ret, v_ret, gate, log_decay.T, q_x, cache_k, cache_v)


def solution(mesh):
    Z, NH = mesh.shape["ctx"] // X, mesh.shape["head"]
    split = P("ctx", "head")
    rows = P(("ctx", "head"), None)
    return jax.shard_map(
        functools.partial(per_device, Z, NH),
        mesh=mesh,
        in_specs=(split,) * 6 + (rows,) * 2,
        out_specs=(split, split),
        check_vma=False,
    )
```

time: 89.2 us -> 61.9 us (0.69)
  the two profiles are of different devices: /device:TPU:448 before, /device:TPU:482 now
where the time goes in v2:
time: 61.9 us; the launch traced here: 61.8 us
  Pallas kernels  58.8 us (95%)
  local copies, waits for them, and re-layouts  2.26 us (4%)
  between operations  0.65 us (1%)
    pallas_call x1, Pallas kernels, per_device(): pl.pallas_call(functools.partial(kernel, Z, NH, T), out_shape=(out, out),...  58.8 us
    unnamed x4, local copies, waits for them, and re-layouts  2.26 us

profile of v2, /device:TPU:482, one launch (start us, length us, event | category | flops | bytes accessed | tf_op | source)
XLA Modules:
  0.0 61.8 jit_solution(411106174428241792)
XLA Ops:
  0.6 58.8 %block.1 = (bf16[128,512]{1,0:T(8,128)(2,1)}, bf16[128,512]{1,0:T(8,128)(2,1)}) custom-call(bf16[128,512]{1,0:T(8,128)(2,1)} %q_ret.1, bf16[128,512]{1,0:T(8,128)(2,1)} %k_ret.1, bf16[128,512]{1,0:T(8,128)(2,1)} %v_ret.1, bf16[128,512]{1,0:T(8,128)(2,1)} %gate.1, f32[2,128]{1,0:T(2,128)} %bitcast.1, bf16[128,512]{1,0:T(8,128)(2,1)} %q_x.1, ...), custom_call_target="tpu_custom_call" | custom-call | tf_op jit(solution)/shard_map/block/pallas_call | solution.py:508
  59.5 0.0 copy-start
  59.5 1.6 %copy.12 = bf16[128,512]{1,0:T(8,128)(2,1)} copy(bf16[128,512]{1,0:T(8,128)(2,1)} %get-tuple-element.4) | data formatting | bytes 262144
  61.1 0.0 copy-done
  61.1 0.7 %copy.13 = bf16[128,512]{1,0:T(8,128)(2,1)} copy(bf16[128,512]{1,0:T(8,128)(2,1)S(1)} %copy-done) | data formatting | bytes 262144
Async XLA Ops:
  59.5 1.6 %copy-start = (bf16[128,512]{1,0:T(8,128)(2,1)S(1)}, bf16[128,512]{1,0:T(8,128)(2,1)}, u32[]{:S(2)}) copy-start(bf16[128,512]{1,0:T(8,128)(2,1)} %get-tuple-element.5) | copy-start | bytes 393220

commit v3 on v2

v3 whole, which is shorter than its diff:
```python
import functools
import math

import jax
import jax.numpy as jnp
from jax import lax
from jax.experimental import pallas as pl
from jax.experimental.pallas import tpu as pltpu
from jax.sharding import PartitionSpec as P

HD = 256
X = 4
NEG = -1e30
EPS = 1e-06
MESH = pl.DeviceIdType.MESH
bf16, f32 = jnp.bfloat16, jnp.float32
SCALE2 = math.log2(math.e) / math.sqrt(HD)
NT = (((1,), (1,)), ((), ()))
TN = (((0,), (0,)), ((), ()))


def mm(a, b, dims=(((1,), (0,)), ((), ()))):
    return lax.dot_general(a, b, dims, preferred_element_type=f32)


def wide(a):
    return jnp.concatenate([a, a], axis=1)


def kernel(
    Z, NH, T,
    q_ret, k_ret, v_ret, gate, ld, q_x, cache_k, cache_v,
    o_ret, o_x,
    qv, kvv, vv, gv, ldv, cv, ox_v, or_v,
    qbuf, own, kv, gown, gsingle, gpair, gbuf, m_s, l_s, acc, o_send, o_recv, st_send, st_recv,
    d_s, within, silu, sum_send, sum_recv, t_send, t_recv, qr, s_f, s_b, e_f,
    fb_send, fb_recv,
    loc_sem, c_send, c_recv, x_send, x_recv, z_send, z_recv, g_send, g_recv,
):
    F = Z // 2 - 1
    B = Z - 1 - F
    STEPS = max(F, B)
    FG = Z // 2
    BG = Z - 1 - FG
    RP = T // NH
    HALF = HD // 2
    c = lax.axis_index("ctx")
    h = lax.axis_index("head")
    z = lax.div(c, X)
    x = lax.rem(c, X)
    odd = lax.rem(z, 2)
    plane = z * X

    def xdev(r):
        xp = lax.rem(x + r, X)
        return xp, (plane + xp, h)

    def hdev(r):
        hp = lax.rem(h + r, NH)
        return hp, (c, hp)

    up = (lax.rem(c + X, Z * X), h)
    down = (lax.rem(c + (Z - 1) * X, Z * X), h)

    def remote(src, dst, ss, rs, dev):
        return pltpu.make_async_remote_copy(
            src_ref=src, dst_ref=dst, send_sem=ss, recv_sem=rs,
            device_id=dev, device_id_type=MESH,
        )

    barrier = pltpu.get_barrier_semaphore()
    for r in range(1, NH):
        pl.semaphore_signal(barrier, inc=1, device_id=hdev(r)[1], device_id_type=MESH)
    for r in range(1, X):
        pl.semaphore_signal(barrier, inc=1, device_id=xdev(r)[1], device_id_type=MESH)
    pl.semaphore_signal(barrier, inc=1, device_id=up, device_id_type=MESH)
    pl.semaphore_signal(barrier, inc=1, device_id=down, device_id_type=MESH)

    def head_cols(i):
        return pl.ds(pl.multiple_of(i * HD, HD), HD)

    my_rows = pl.ds(pl.multiple_of(h * RP, RP), RP)
    pairs = (
        (ld, ldv), (k_ret, kvv), (v_ret, vv),
        (cache_k, cv.at[0]), (cache_v, cv.at[1]),
        (q_x.at[:, 0:HD], qbuf.at[x, 0]),
        (q_x.at[:, HD:2 * HD], qbuf.at[x, 1]),
        (cache_k.at[:, head_cols(h)], own.at[0, my_rows]),
        (cache_v.at[:, head_cols(h)], own.at[1, my_rows]),
        (q_ret, qv), (gate, gv),
        (q_ret.at[:, head_cols(lax.div(x, 2))], qr.at[x]),
    )
    local = [pltpu.make_async_copy(src, dst, loc_sem.at[n]) for n, (src, dst) in enumerate(pairs)]
    for n in (3, 4, 0, 1, 2, 5, 6, 7, 8, 9, 10, 11):
        local[n].start()

    def cache_copy(r, t):
        hp, dev = hdev(r)
        return remote(cv.at[t, :, head_cols(hp)], own.at[t, my_rows], c_send.at[t, r], c_recv.at[t, r], dev)

    def x_copy(kind, r):
        xp, dev = xdev(r)
        if kind == 0:
            src, dst = sum_send.at[xp], sum_recv.at[x]
        elif kind == 1:
            src, dst = t_send, t_recv.at[x]
        elif kind == 2 or kind == 3:
            src, dst = qbuf.at[x, kind - 2], qbuf.at[x, kind - 2]
        elif kind == 4:
            src, dst = q_ret.at[:, head_cols(lax.div(xp, 2))], qr.at[x]
        elif kind == 5:
            src, dst = o_send.at[xp], o_recv.at[x]
        elif kind == 6:
            src, dst = st_send.at[xp], st_recv.at[x]
        else:
            src, dst = fb_send.at[xp], fb_recv.at[x]
        return remote(src, dst, x_send.at[kind, r], x_recv.at[kind, r], dev)

    order = (2, 1, 3)
    for n in (3, 4):
        local[n].wait()
    pl.semaphore_wait(barrier, (NH - 1) + (X - 1) + 2)
    for t in range(2):
        for r in range(1, NH):
            cache_copy(r, t).start()

    for n in (0, 1, 2):
        local[n].wait()
    lane8 = lax.broadcasted_iota(jnp.int32, (8, T), 1)
    for hh in range(2):
        dr = jnp.broadcast_to(ldv[hh:hh + 1, :], (8, T))
        step = 1
        while step < T:
            dr = dr + jnp.where(lane8 >= step, pltpu.roll(dr, step, 1), 0.0)
            step *= 2
        d = jnp.concatenate([dr] * (T // 8), axis=0).T
        d_s[hh] = d
        last = d[T - 1:T, :]
        fade = jnp.exp(last - d)
        kh = kvv[:, hh * HD:(hh + 1) * HD]
        vh = vv[:, hh * HD:(hh + 1) * HD]
        carried = (kh.astype(f32) * wide(fade)).astype(bf16)
        summ = mm(carried, vh, TN).astype(bf16)
        sum_send[2 * hh] = summ[:, :HALF]
        sum_send[2 * hh + 1] = summ[:, HALF:]
        t_send[4 * hh:4 * hh + 4, :] = jnp.broadcast_to(last, (4, T))
    for kind in (1, 0):
        for r in order:
            x_copy(kind, r).start()
    for n in (5, 6):
        local[n].wait()
    for kind in (2, 3, 4):
        for r in order:
            x_copy(kind, r).start()

    def way_dev(way):
        return up if way == 0 else down

    PT = T // 2

    def piece(t):
        return t // 2, pl.ds((t % 2) * PT, PT)

    def mine(t):
        return own.at[piece(t)[0], piece(t)[1]]

    def slot(t, way, i):
        return kv.at[piece(t)[0], way, i, piece(t)[1]]

    def send_own(t, way):
        return remote(mine(t), slot(t, way, 0), z_send.at[t, way, 0], z_recv.at[t, way, 0], way_dev(way))

    low = z < STEPS
    back_shift = jnp.where(low, 1, 0)
    back_lag = jnp.where(low, 0, Z - 1 - z)

    def pass_on(t, way, i):
        to = i + 1 if way == 0 else i + back_shift
        return remote(slot(t, way, i), slot(t, way, to), z_send.at[t, way, i + 1], z_recv.at[t, way, to], way_dev(way))

    def arrival(t, way, i):
        return remote(mine(t), slot(t, way, i), z_send.at[t, way, 0], z_recv.at[t, way, i], way_dev(way))

    own_up = z < Z - 1
    own_down = z < B
    got_up = jnp.minimum(z, F)
    got_down = jnp.where(low, jnp.maximum(B - 1 - z, 0), jnp.maximum(z - F, 0))
    use_down = jnp.where(low, 0, jnp.maximum(z - F, 0))
    pass_up = jnp.where(own_up, jnp.minimum(z, F - 1), 0)
    pass_down = jnp.where(low, got_down, jnp.maximum(z - F - 1, 0))

    def relay(t, s):
        for way in range(2):
            i = s if way == 0 else s - back_lag
            got, passed = (got_up, pass_up) if way == 0 else (got_down, pass_down)

            @pl.when(jnp.logical_and(i >= 0, i < got))
            def _():
                arrival(t, way, i).wait_recv()

            @pl.when(jnp.logical_and(i >= 0, i < passed))
            def _():
                pass_on(t, way, i).start()

    def start_own(t):
        local[7 + t].wait()
        for r in range(1, NH):
            cache_copy(r, t).wait_recv()
        for p in (2 * t, 2 * t + 1):
            @pl.when(own_up)
            def _():
                send_own(p, 0).start()

            @pl.when(own_down)
            def _():
                send_own(p, 1).start()

    start_own(0)

    sum_recv[x] = sum_send[x]
    t_recv[x] = t_send[...]
    s_f[...] = jnp.zeros_like(s_f)
    s_b[...] = jnp.zeros_like(s_b)
    e_f[...] = jnp.zeros_like(e_f)
    def local_part():
        local[9].wait()
        local[10].wait()
        rows = lax.broadcasted_iota(jnp.int32, (T, T), 0)
        cols = lax.broadcasted_iota(jnp.int32, (T, T), 1)
        for hh in range(2):
            d = d_s[hh]
            qh = qv[:, hh * HD:(hh + 1) * HD]
            kh = kvv[:, hh * HD:(hh + 1) * HD]
            vh = vv[:, hh * HD:(hh + 1) * HD]
            spread = jnp.minimum(d - d.T, 0.0)
            w = jnp.where(rows >= cols, jnp.exp(spread) * mm(qh, kh, NT), 0.0).astype(bf16)
            within[hh] = mm(w, vh)
            g = gv[:, hh * HD:(hh + 1) * HD].astype(f32)
            silu[hh] = g / (1.0 + jnp.exp(-g))

    def attend(kb, vb, first):
        k = kb[...]
        v = vb[...]
        for i in range(X):
            q = qbuf[i].reshape(2 * T, HD)
            at = pl.ds(i * 2 * T, 2 * T)
            s = mm(q, k, NT)
            if first:
                t_pos = lax.rem(lax.broadcasted_iota(jnp.int32, (2 * T, T), 0), T)
                ok = t_pos + (i - x) * T >= lax.broadcasted_iota(jnp.int32, (2 * T, T), 1)
                s = jnp.where(ok, s, NEG)
                m_new = jnp.broadcast_to(jnp.max(s, axis=1, keepdims=True), (2 * T, T))
                p = jnp.where(ok, jnp.exp2((s - m_new) * SCALE2), 0.0)
                l_s[at, :] = p
                acc[at, :] = mm(p.astype(bf16), v)
            else:
                m_old = m_s[at, :]
                m_new = jnp.maximum(m_old, jnp.max(s, axis=1, keepdims=True))
                p = jnp.exp2((s - m_new) * SCALE2)
                alpha = jnp.exp2((m_old - m_new) * SCALE2)
                l_s[at, :] = l_s[at, :] * alpha + p
                acc[at, :] = acc[at, :] * wide(alpha) + mm(p.astype(bf16), v)
            m_s[at, :] = m_new

    def attend_slot(way, n):
        i = n if way == 0 else n - back_lag

        @pl.when(jnp.logical_and(i >= 0, i < (got_up if way == 0 else use_down)))
        def _():
            attend(kv.at[0, way, i], kv.at[1, way, i], False)


    for kind in (1, 0):
        for r in order:
            x_copy(kind, r).wait_recv()

    second = lax.div(x, 2) == 1

    def total(i):
        tr = t_recv[i]
        return jnp.where(second, tr[4:5, :], tr[0:1, :])

    tail_rows = lax.broadcasted_iota(jnp.int32, (16, HALF), 0)

    def pack(ref, value, decay):
        ref[0:HD, :] = value.astype(bf16)
        hi = decay.astype(bf16).astype(f32)
        mid = (decay - hi).astype(bf16).astype(f32)
        lowest = decay - hi - mid
        rest = jnp.where(tail_rows == 0, hi, jnp.where(tail_rows == 1, mid, jnp.where(tail_rows == 2, lowest, 0.0)))
        ref[HD:HD + 16, :] = rest.astype(bf16)

    def unpack(ref):
        tail = ref[HD:HD + 16, :].astype(f32)
        return ref[0:HD, :].astype(f32), tail[0:1, :] + tail[1:2, :] + tail[2:3, :]

    g_own = sum_recv[0].astype(f32)
    g_decay = total(0)
    for i in range(1, X):
        g_own = g_own * jnp.exp(total(i)) + sum_recv[i].astype(f32)
        g_decay = g_decay + total(i)

    cut = (pl.ds(0, HALF), pl.ds(HALF, HALF + 16))

    def single(p):
        return remote(gown.at[cut[p]], gsingle.at[cut[p]], g_send.at[p, 0, FG], g_recv.at[p, 0, FG], up)

    @pl.when(odd == 0)
    def _():
        pack(gown, g_own, g_decay)
        for p in range(2):
            single(p).start()

    start_own(1)

    def pair_own(way, p):
        return remote(gpair.at[cut[p]], gbuf.at[way, 0, cut[p]], g_send.at[p, way, FG + 1], g_recv.at[p, way, 0], way_dev(way))

    def pair_pass(way, k, p):
        to = jnp.where(low, k + odd, k) if way == 1 else k + odd
        return remote(gbuf.at[way, k, cut[p]], gbuf.at[way, to, cut[p]], g_send.at[p, way, k], g_recv.at[p, way, to], way_dev(way))

    pair_up = jnp.logical_and(odd == 1, own_up)
    pair_down = jnp.logical_and(odd == 1, z < BG)
    g_up = jnp.minimum(lax.div(z, 2), jnp.where(odd == 1, FG // 2, (FG + 1) // 2))
    g_down = jnp.where(low, jnp.maximum(BG // 2 - lax.div(z + 1, 2), 0), lax.div(jnp.maximum(z - FG, 0), 2))
    g_pass_up = jnp.where(own_up, jnp.minimum(g_up, jnp.where(odd == 1, (FG - 1) // 2, FG // 2)), 0)
    g_pass_down = jnp.where(low, g_down, lax.div(jnp.maximum(z - 1 - FG, 0), 2))

    def pair_relay(dist):
        for way in range(2):
            if way == 0:
                off = dist - 1 - odd
                got, passed = g_up, g_pass_up
            else:
                off = dist - 1 - jnp.where(low, odd, Z - z)
                got, passed = g_down, g_pass_down
            k = lax.div(jnp.maximum(off, 0), 2)
            here = jnp.logical_and(off >= 0, lax.rem(jnp.maximum(off, 0), 2) == 0)

            for p in range(2):
                @pl.when(jnp.logical_and(here, k < got))
                def _():
                    remote(gpair.at[cut[p]], gbuf.at[way, k, cut[p]], g_send.at[p, way, FG + 1], g_recv.at[p, way, k], way_dev(way)).wait_recv()

                @pl.when(jnp.logical_and(here, k < passed))
                def _():
                    pair_pass(way, k, p).start()

            if way == 0:
                @pl.when(jnp.logical_and(here, k < got))
                def _():
                    g, decay = unpack(gbuf.at[0, k])
                    s_f[...] = s_f[...] + jnp.exp(e_f[0:1, :]) * g
                    e_f[...] = e_f[...] + decay
            else:
                @pl.when(jnp.logical_and(here, jnp.logical_and(k < got, z > FG)))
                def _():
                    g, decay = unpack(gbuf.at[1, k])
                    s_b[...] = s_b[...] * jnp.exp(decay) + g

    relay(0, 0)
    relay(1, 0)

    @pl.when(odd == 1)
    def _():
        for p in range(2):
            single(p).wait_recv()
        g_before, d_before = unpack(gsingle)
        s_f[...] = g_before
        e_f[...] = e_f[...] + d_before
        pack(gpair, g_before * jnp.exp(g_decay) + g_own, d_before + g_decay)

    @pl.when(pair_up)
    def _():
        for p in range(2):
            pair_own(0, p).start()

    @pl.when(pair_down)
    def _():
        for p in range(2):
            pair_own(1, p).start()

    relay(2, 0)
    relay(3, 0)
    for t in range(4):
        relay(t, 1)
    for kind in (2, 3):
        for r in order:
            x_copy(kind, r).wait_recv()
    attend(own.at[0], own.at[1], True)

    def reach(s):
        return jnp.where(s < 2, 0, jnp.where(s == 2, 1, s))

    def attend_slots(way, lo, hi):
        def one(n, carry):
            attend_slot(way, n)
            return carry

        lax.fori_loop(lo, hi, one, 0)

    def step(s, carry):
        lo, hi = reach(s - 1), reach(s)
        relay(0, s)
        relay(1, s)
        pair_relay(s - 1)
        attend_slots(0, lo, hi)
        relay(2, s)
        relay(3, s)
        attend_slots(1, lo, hi)
        return carry

    lax.fori_loop(2, STEPS, step, 0)
    for way in range(2):
        attend_slots(way, reach(jnp.int32(STEPS - 1)), STEPS)

    lane = lax.broadcasted_iota(jnp.int32, (T, T), 1)
    for r in order:
        xp, _ = xdev(r)
        stat = jnp.zeros((T, T), f32)
        for hh in range(2):
            at = pl.ds(pl.multiple_of((xp * 2 + hh) * T, T), T)
            l = jnp.sum(l_s[at, :], axis=1, keepdims=True)
            o_send[xp, hh] = (acc[at, :] * (1.0 / jnp.where(l > 0.0, l, 1.0))).astype(bf16)
            stat = jnp.where(lane == 2 * hh, m_s[at, :], stat)
            stat = jnp.where(lane == 2 * hh + 1, l, stat)
        st_send[xp] = stat.T[0:8, :]
        x_copy(6, r).start()
        x_copy(5, r).start()

    for dist in range(STEPS - 1, FG + 1):
        pair_relay(jnp.int32(dist))

    local[11].wait()
    for r in order:
        x_copy(4, r).wait_recv()
    state = s_f[...] + jnp.exp(e_f[0:1, :]) * s_b[...]
    for i in range(X):
        top = state.astype(bf16)
        low_part = (state - top.astype(f32)).astype(bf16)
        fb_send[i] = (mm(qr[i], top) + mm(qr[i], low_part)).astype(bf16)
        if i < X - 1:
            state = state * jnp.exp(total(i)) + sum_recv[i].astype(f32)
    for r in order:
        x_copy(7, r).start()

    local_part()

    stats = {}
    for r in order:
        x_copy(6, r).wait_recv()
        xp, _ = xdev(X - r)
        stats[r] = (xp, jnp.concatenate([st_recv[xp]] * (T // 8), axis=0).T)
    joined = []
    for hh in range(2):
        at = pl.ds(pl.multiple_of((x * 2 + hh) * T, T), T)
        m_own = m_s[at, :][:, 0:1]
        l_own = jnp.sum(l_s[at, :], axis=1, keepdims=True)
        top = m_own
        for r in order:
            top = jnp.maximum(top, stats[r][1][:, 2 * hh:2 * hh + 1])
        w_own = jnp.exp2((m_own - top) * SCALE2)
        weight = l_own * w_own
        shares = {}
        for r in order:
            st = stats[r][1]
            shares[r] = jnp.exp2((st[:, 2 * hh:2 * hh + 1] - top) * SCALE2) * st[:, 2 * hh + 1:2 * hh + 2]
            weight = weight + shares[r]
        inv = 1.0 / weight
        joined.append((at, w_own * inv, {r: shares[r] * inv for r in order}))
    outs = [acc[at, :] * w_own for at, w_own, _ in joined]
    for r in (1, 3, 2):
        x_copy(5, r).wait_recv()
        xp = stats[r][0]
        for hh in range(2):
            outs[hh] = outs[hh] + o_recv[xp, hh].astype(f32) * joined[hh][2][r]
    for hh in range(2):
        ox_v[:, hh * HD:(hh + 1) * HD] = outs[hh].astype(bf16)
    out_copies = [pltpu.make_async_copy(ox_v, o_x, loc_sem.at[12]), pltpu.make_async_copy(or_v, o_ret, loc_sem.at[13])]
    out_copies[0].start()

    for r in order:
        x_copy(7, r).wait_recv()
    fb_recv[x] = fb_send[x]
    for hh in range(2):
        d = jnp.exp(d_s[hh])
        before = jnp.concatenate([fb_recv[2 * hh], fb_recv[2 * hh + 1]], axis=1).astype(f32)
        kept = within[hh] + wide(d) * before
        normed = kept * lax.rsqrt(jnp.mean(kept * kept, axis=1, keepdims=True) + EPS)
        or_v[:, hh * HD:(hh + 1) * HD] = (normed * silu[hh]).astype(bf16)
    out_copies[1].start()

    for r in range(1, NH):
        for t in range(2):
            cache_copy(r, t).wait_send()
    for kind in range(8):
        for r in order:
            x_copy(kind, r).wait_send()
    for t in range(4):
        @pl.when(own_up)
        def _():
            send_own(t, 0).wait_send()

        @pl.when(own_down)
        def _():
            send_own(t, 1).wait_send()

    @pl.when(odd == 0)
    def _():
        for p in range(2):
            single(p).wait_send()

    @pl.when(pair_up)
    def _():
        for p in range(2):
            pair_own(0, p).wait_send()

    @pl.when(pair_down)
    def _():
        for p in range(2):
            pair_own(1, p).wait_send()

    def drain(i, carry):
        for way, passed, g_passed in ((0, pass_up, g_pass_up), (1, pass_down, g_pass_down)):
            for t in range(4):
                @pl.when(i < passed)
                def _():
                    pass_on(t, way, i).wait_send()

            @pl.when(i < g_passed)
            def _():
                for p in range(2):
                    pair_pass(way, i, p).wait_send()
        return carry

    lax.fori_loop(0, STEPS, drain, 0)
    for cp in out_copies:
        cp.wait()


def per_device(Z, NH, q_ret, k_ret, v_ret, gate, log_decay, q_x, cache_k, cache_v):
    T = q_ret.shape[0]
    F = Z // 2
    W = HD // 2
    vm = pltpu.VMEM
    dma = pltpu.SemaphoreType.DMA
    out = jax.ShapeDtypeStruct((T, 2 * HD), bf16)
    item = (HD + 16, W)
    return pl.pallas_call(
        functools.partial(kernel, Z, NH, T),
        out_shape=(out, out),
        in_specs=[pl.BlockSpec(memory_space=pl.ANY)] * 8,
        out_specs=(pl.BlockSpec(memory_space=pl.ANY),) * 2,
        scratch_shapes=[
            vm((T, 2 * HD), bf16), vm((T, 2 * HD), bf16), vm((T, 2 * HD), bf16), vm((T, 2 * HD), bf16), vm((2, T), f32), vm((2, T // NH, NH * HD), bf16),
            vm((T, 2 * HD), bf16), vm((T, 2 * HD), bf16),
            vm((X, 2, T, HD), bf16), vm((2, T, HD), bf16), vm((2, 2, F, T, HD), bf16),
            vm(item, bf16), vm(item, bf16), vm(item, bf16), vm((2, F // 2 + 1) + item, bf16),
            vm((X * 2 * T, T), f32), vm((X * 2 * T, T), f32), vm((X * 2 * T, HD), f32),
            vm((X, 2, T, HD), bf16), vm((X, 2, T, HD), bf16), vm((X, 8, T), f32), vm((X, 8, T), f32),
            vm((2, T, T), f32), vm((2, T, HD), f32), vm((2, T, HD), f32),
            vm((4, HD, W), bf16), vm((X, HD, W), bf16), vm((8, T), f32), vm((X, 8, T), f32),
            vm((X, T, HD), bf16), vm((HD, W), f32), vm((HD, W), f32), vm((8, T), f32),
            vm((X, T, W), bf16), vm((X, T, W), bf16),
            dma((14,)), dma((2, NH)), dma((2, NH)), dma((8, X)), dma((8, X)),
            dma((4, 2, F + 1)), dma((4, 2, F + 1)), dma((2, 2, F + 2)), dma((2, 2, F + 2)),
        ],
        compiler_params=pltpu.CompilerParams(collective_id=0, has_side_effects=True),
        name="block",
    )(q_ret, k_ret, v_ret, gate, log_decay.T, q_x, cache_k, cache_v)


def solution(mesh):
    Z, NH = mesh.shape["ctx"] // X, mesh.shape["head"]
    split = P("ctx", "head")
    rows = P(("ctx", "head"), None)
    return jax.shard_map(
        functools.partial(per_device, Z, NH),
        mesh=mesh,
        in_specs=(split,) * 6 + (rows,) * 2,
        out_specs=(split, split),
        check_vma=False,
    )
```

time: 61.9 us -> 59.1 us (0.955)
  the two profiles are of different devices: /device:TPU:482 before, /device:TPU:1 now
where the time goes in v3:
time: 59.1 us; the launch traced here: 58.2 us
  Pallas kernels  55.3 us (94%)
  local copies, waits for them, and re-layouts  2.26 us (4%)
  between operations  0.65 us (1%)
    pallas_call x1, Pallas kernels, per_device(): pl.pallas_call(functools.partial(kernel, Z, NH, T), out_shape=(out, out),...  55.3 us
    unnamed x4, local copies, waits for them, and re-layouts  2.26 us

profile of v3, /device:TPU:1, one launch (start us, length us, event | category | flops | bytes accessed | tf_op | source)
XLA Modules:
  0.0 58.2 jit_solution(8165002747578302299)
XLA Ops:
  0.6 55.3 %block.1 = (bf16[128,512]{1,0:T(8,128)(2,1)}, bf16[128,512]{1,0:T(8,128)(2,1)}) custom-call(bf16[128,512]{1,0:T(8,128)(2,1)} %q_ret.1, bf16[128,512]{1,0:T(8,128)(2,1)} %k_ret.1, bf16[128,512]{1,0:T(8,128)(2,1)} %v_ret.1, bf16[128,512]{1,0:T(8,128)(2,1)} %gate.1, f32[2,128]{1,0:T(2,128)} %bitcast.1, bf16[128,512]{1,0:T(8,128)(2,1)} %q_x.1, ...), custom_call_target="tpu_custom_call" | custom-call | tf_op jit(solution)/shard_map/block/pallas_call | solution.py:550
  56.0 0.0 copy-start
  56.0 1.6 %copy.12 = bf16[128,512]{1,0:T(8,128)(2,1)} copy(bf16[128,512]{1,0:T(8,128)(2,1)} %get-tuple-element.4) | data formatting | bytes 262144
  57.6 0.0 copy-done
  57.6 0.7 %copy.13 = bf16[128,512]{1,0:T(8,128)(2,1)} copy(bf16[128,512]{1,0:T(8,128)(2,1)S(1)} %copy-done) | data formatting | bytes 262144
Async XLA Ops:
  56.0 1.6 %copy-start = (bf16[128,512]{1,0:T(8,128)(2,1)S(1)}, bf16[128,512]{1,0:T(8,128)(2,1)}, u32[]{:S(2)}) copy-start(bf16[128,512]{1,0:T(8,128)(2,1)} %get-tuple-element.5) | copy-start | bytes 393220
